TPU v7x, 32 devices: a whole 2x2x4 slice. The times are simulated.
32 devices in a mesh: line: 8 (over z, y), bus: 4 (over x, core).
Axes of the slice: x: 2, y: 2, z: 4, core: 2. Of those that a mesh axis runs over, the one named last changes fastest.
Arguments:
- clearness: float32 [192, 8192], P(None, ('line', 'bus')), may hold values from 0.05 to 0.8
- cos_zenith: float32 [192, 8192], P(None, ('line', 'bus')), may hold values from 0.05 to 1
- sun_azimuth: float32 [192, 8192], P(None, ('line', 'bus')), may hold values from -3.140625 to 3.140625
- dirint_cell: int32 [192, 8192], P(None, ('line', 'bus')), may hold values from 0 to 1259
- sky_bin: int32 [192, 8192], P(None, ('line', 'bus')), may hold values from 0 to 7
- dirint_coef: float32 [1260], replicated, may hold values from 0.5 to 1.5
- perez_coef: float32 [6, 8], replicated, may hold values from -0.3 to 0.6
- tilt_class: int32 [8192], P(('line', 'bus')), may hold values from 0 to 7
- azimuth_class: int32 [8192], P(('line', 'bus')), may hold values from 0 to 11
- tilt_table: float32 [8], replicated, may hold values from 0 to 1
- azimuth_table: float32 [12], replicated, may hold values from -3.140625 to 3.140625
- capacity: float32 [8192], P(('line', 'bus')), may hold values from 0.2 to 2
- site_bus: int32 [8192], P(('line', 'bus')), may hold values from 0 to 70143, as said below
- transfer_factors: bfloat16 [16000, 70144], P('line', 'bus'), may hold values from -0.0234375 to 0.0234375
Outputs:
- flows: float32 [16000, 192], P('line', 'bus')
Inputs may be any that keep to these rules, and one draw needn't show every extreme that they name: `site_bus`: bus b lies in group b // 2192. In every aligned block of 256 sites at most 16 sites connect to buses of one group, and one group receives exactly 16 sites from every block.
All inputs are finite; a program needn't handle non-finite values.
Results may differ from a plain program's by a relative error of at most 0.0034.
Values may be sent and summed in bfloat16 or wider, within the bound.
No kernel may reach another device: no remote copies, remote signals or barrier semaphores. Data moves between devices by JAX's collectives and lax.ppermute only.
A program may use at most 128 MiB of HBM per device.

v0:
```python
import math
import jax
import jax.numpy as jnp
from jax import lax
from jax.sharding import PartitionSpec as P

BUSES = 70144
TILTS = 8
AZIMS = 12
solar_constant = 1367.0
albedo = 0.2
cos_limit = 0.08716
row_width = 36


def pick_table(classes, table, count):
    picked = jnp.zeros(classes.shape, jnp.float32)
    for entry in range(count):
        picked = jnp.where(classes == entry, table[entry], picked)
    return picked


def dirint_lookup(cell, dirint_coef):
    row_count = dirint_coef.shape[0] // row_width
    table = dirint_coef.reshape(row_count, row_width)
    flat_cell = cell.reshape(-1)
    upper = flat_cell // row_width
    lower = flat_cell % row_width
    row_pick = (upper[:, None] == jnp.arange(row_count, dtype=jnp.int32)[None, :]).astype(
        jnp.float32
    )
    rows = jnp.dot(
        row_pick, table, precision=lax.Precision.HIGHEST, preferred_element_type=jnp.float32
    )
    column_hit = lower[:, None] == jnp.arange(row_width, dtype=jnp.int32)[None, :]
    picked = jnp.sum(jnp.where(column_hit, rows, 0.0), axis=1)
    return picked.reshape(cell.shape)


def site_power(
    clear,
    cosz,
    sun_az,
    cell,
    sky,
    tilt_angle,
    array_azimuth,
    site_capacity,
    dirint_coef,
    perez_coef,
):
    global_flat = clear * solar_constant * cosz
    zenith = jnp.arccos(cosz)
    airmass = 1.0 / (cosz + 0.50572 * (96.07995 - zenith * (180.0 / math.pi)) ** (-1.6364))
    clear_beam = (
        0.866 - 0.122 * airmass + 0.0121 * airmass**2 - 0.000653 * airmass**3 + 1.4e-05 * airmass**4
    )
    part_a = 0.512 - 1.56 * clear + 2.286 * clear**2 - 2.222 * clear**3
    part_b = 0.37 + 0.962 * clear
    part_c = -0.28 + 0.932 * clear - 2.048 * clear**2
    beam_index = jnp.maximum(clear_beam - (part_a + part_b * jnp.exp(part_c * airmass)), 0.0)
    direct_normal = solar_constant * beam_index * dirint_lookup(cell, dirint_coef)
    diffuse = jnp.maximum(global_flat - direct_normal * cosz, 0.1 * global_flat)
    brightness = diffuse * airmass / solar_constant
    factors = [jnp.zeros(cosz.shape, jnp.float32) for entry in range(6)]
    for bin_index in range(perez_coef.shape[1]):
        hit = sky == bin_index
        factors = [jnp.where(hit, perez_coef[row, bin_index], factors[row]) for row in range(6)]
    circumsolar = jnp.maximum(0.0, factors[0] + factors[1] * brightness + factors[2] * zenith)
    horizon_term = factors[3] + factors[4] * brightness + factors[5] * zenith
    cos_tilt = jnp.cos(tilt_angle)
    sin_tilt = jnp.sin(tilt_angle)
    cos_incidence = cosz * cos_tilt + jnp.sin(zenith) * sin_tilt * jnp.cos(sun_az - array_azimuth)
    facing = jnp.maximum(cos_incidence, 0.0)
    horizon_cos = jnp.maximum(cosz, cos_limit)
    sky_part = diffuse * (
        (1.0 - circumsolar) * (1.0 + cos_tilt) * 0.5
        + circumsolar * facing / horizon_cos
        + horizon_term * sin_tilt
    )
    plane = direct_normal * facing + sky_part + albedo * global_flat * (1.0 - cos_tilt) * 0.5
    return (site_capacity * plane / 1000.0).astype(jnp.bfloat16)


def per_device(
    clearness,
    cos_zenith,
    sun_azimuth,
    dirint_cell,
    sky_bin,
    dirint_coef,
    perez_coef,
    tilt_class,
    azimuth_class,
    tilt_table,
    azimuth_table,
    capacity,
    site_bus,
    transfer_factors,
):
    line_count = lax.axis_size("line")
    bus_count = lax.axis_size("bus")
    owners = line_count * bus_count
    n_hours, n_sites = clearness.shape
    group_buses = BUSES // owners
    slots_each = max(2, 2 * n_sites // owners)
    tilt_angle = pick_table(tilt_class, tilt_table, TILTS)
    array_azimuth = pick_table(azimuth_class, azimuth_table, AZIMS)
    power = site_power(
        clearness,
        cos_zenith,
        sun_azimuth,
        dirint_cell,
        sky_bin,
        tilt_angle,
        array_azimuth,
        capacity,
        dirint_coef,
        perez_coef,
    )
    group_index = site_bus // group_buses
    target = group_index % line_count * bus_count + group_index // line_count
    local_bus = site_bus % group_buses
    one_hot = (target[:, None] == jnp.arange(owners, dtype=jnp.int32)[None, :]).astype(jnp.int32)
    position = jnp.sum(one_hot * (jnp.cumsum(one_hot, axis=0) - 1), axis=1)
    slot_index = target * slots_each + position
    outgoing = jnp.zeros((n_hours, owners * slots_each), jnp.bfloat16).at[:, slot_index].set(power)
    labels = jnp.zeros((1, owners * slots_each), jnp.int32).at[0, slot_index].set(local_bus)
    arrived, bus_tags = (
        lax.all_to_all(outgoing, ("line", "bus"), split_axis=1, concat_axis=1, tiled=True),
        lax.all_to_all(labels, ("line", "bus"), split_axis=1, concat_axis=1, tiled=True),
    )
    bus_tags = bus_tags.reshape(owners * slots_each)
    member = (bus_tags[:, None] == jnp.arange(group_buses, dtype=jnp.int32)[None, :]).astype(
        jnp.bfloat16
    )
    injection = jnp.einsum("hr,rb->bh", arrived, member, preferred_element_type=jnp.float32).astype(
        jnp.bfloat16
    )
    partial_flows = jnp.dot(
        transfer_factors,
        lax.all_gather(injection, "line", axis=0, tiled=True),
        preferred_element_type=jnp.float32,
    )
    return lax.psum_scatter(partial_flows, "bus", scatter_dimension=1, tiled=True)


def solution(mesh):
    in_specs = (
        P(None, ("line", "bus")),
        P(None, ("line", "bus")),
        P(None, ("line", "bus")),
        P(None, ("line", "bus")),
        P(None, ("line", "bus")),
        P(),
        P(),
        P(("line", "bus")),
        P(("line", "bus")),
        P(),
        P(),
        P(("line", "bus")),
        P(("line", "bus")),
        P("line", "bus"),
    )
    out_specs = P("line", "bus")
    return jax.shard_map(
        per_device, mesh=mesh, in_specs=in_specs, out_specs=out_specs, check_vma=False
    )
```

profile of v0, /device:TPU:0, one launch (start us, length us, event | category | flops | bytes accessed | tf_op | source)
XLA Modules:
  0.0 296.3 jit_solution(16229938110226175644)
XLA Ops:
  6.5 0.0 copy-start.2
  6.6 0.8 and_select_fusion
  7.3 0.6 reduce-window.6
  7.9 0.2 slice_reduce_fusion
  8.2 0.1 fusion.27
  8.3 1.4 scatter_custom_fusion
  9.7 0.7 all_to_all.14
  10.4 7.3 %all-to-all-start = ((s32[1,32,16]{2,0,1:T(1,128)}), s32[1,32,16]{2,0,1:T(1,128)S(1)}, u32[]{:S(2)}, u32[]{:S(2)}) async-start(s32[1,32,16]{2,0,1:T(1,128)} %bitcast.2), calls=%async_computation | async-start | bytes 32768 | tf_op jit(solution)/shard_map/all_to_all | solution.py:131
  17.7 1.7 fusion.36
  19.4 2.1 fusion.34
  21.5 2.1 fusion.35
  23.6 1.0 sign_compare_fusion
  24.6 1.0 remainder_bitcast_fusion
  25.6 1.6 fusion.38
  27.2 5.7 %fusion.33 = (f32[256]{0:T(256)S(1)}, f32[256]{0:T(256)S(1)}) fusion(f32[]{:T(128)} %bitcast.10, s32[256]{0:T(256)} %param.21, f32[]{:T(128)} %bitcast.9, f32[]{:T(128)} %bitcast.8, f32[]{:T(128)} %bitcast.7, f32[]{:T(128)} %bitcast.6, f32[]{:T(128)} %bitcast.5, f32[]{:T(128)} %bitcast.4, f32[]{:T(128)} %bitcast.3), kind=kLoop, calls=%fused_computation.89 | loop fusion | flops 4096 | bytes 3104 | tf_op jit(solution)/shard_map/sin | solution.py:72
  33.0 1.8 fusion.37
  34.8 0.8 reshape.70
  35.7 0.1 copy.28
  35.8 0.1 copy.29
  35.9 0.1 add_select_fusion.1
  36.0 5.6 %fusion.5 = f32[49152]{0:T(1024)S(1)} fusion(f32[35,36]{1,0:T(8,128)S(1)} %reshape.70, s32[49152]{0:T(1024)S(1)} %get-tuple-element.8, s32[49152]{0:T(1024)S(1)} %get-tuple-element.7), kind=kOutput, calls=%fused_computation.12 | convolution fusion | flops 750157824 | bytes 594864 | tf_op jit(solution)/shard_map/dot_general | solution.py:32
  41.6 0.1 reshape.71
  41.7 0.0 copy-done.4
  41.7 7.5 %broadcast_add_fusion = (f32[256]{0:T(256)S(1)}, f32[256]{0:T(256)S(1)}, f32[256]{0:T(256)S(1)}) fusion(f32[256]{0:T(256)S(1)} %cos.6, f32[]{:T(128)} %bitcast.22, s32[256]{0:T(256)S(1)} %copy-done.4, f32[]{:T(128)} %bitcast.21, f32[]{:T(128)} %bitcast.20, f32[]{:T(128)} %bitcast.19, f32[]{:T(128)} %bitcast.18, f32[]{:T(128)} %bitcast.17, f32[]{:T(128)} %bitcast.16, ...), kind=kLoop, calls=%fused_computation.88 | loop fusion | flops 6912 | bytes 5168 | tf_op jit(solution)/shard_map/add | solution.py:77
  49.2 0.0 copy-done.5
  49.2 0.0 copy-done.1
  49.2 0.0 copy-done.3
  49.2 0.0 copy-done
  49.3 0.0 copy-done.2
  49.3 32.6 %fusion.25 = bf16[256,192]{0,1:T(8,128)(2,1)S(1)} fusion(f32[256]{0:T(256)S(1)} %get-tuple-element.62, f32[]{:T(128)} %bitcast.70, f32[]{:T(128)} %bitcast.69, f32[]{:T(128)} %bitcast.68, f32[]{:T(128)} %bitcast.67, f32[]{:T(128)} %bitcast.66, f32[]{:T(128)} %bitcast.65, f32[]{:T(128)} %bitcast.64, f32[]{:T(128)} %bitcast.63, f32[]{:T(128)} %bitcast.62, ...), kind=kLoop, calls=%fused_computation.45 | loop fusion | flops 6733824 | bytes 1087680 | tf_op jit(solution)/shard_map/convert_element_type | solution.py:82
  81.8 0.1 copy.25
  81.9 2.1 scatter_custom_fusion.1
  84.1 0.0 all-to-all-done
  84.1 5.8 %all-to-all-start.1 = ((bf16[192,32,16]{0,2,1:T(8,128)(2,1)}), bf16[192,32,16]{0,2,1:T(8,128)(2,1)S(1)}, u32[]{:S(2)}, u32[]{:S(2)}) async-start(bf16[192,32,16]{0,2,1:T(8,128)(2,1)} %bitcast.72), calls=%async_computation.1 | async-start | bytes 524288 | tf_op jit(solution)/shard_map/all_to_all | solution.py:130
  89.9 0.0 all-gather.3.cloned.1.call-start
  90.0 0.5 broadcast.198
  90.5 0.7 reduce.5
  91.2 0.1 eq.192
  91.3 9.2 %all-to-all-done.1 = bf16[192,32,16]{0,2,1:T(8,128)(2,1)S(1)} async-done(((bf16[192,32,16]{0,2,1:T(8,128)(2,1)}), bf16[192,32,16]{0,2,1:T(8,128)(2,1)S(1)}, u32[]{:S(2)}, u32[]{:S(2)}) %all-to-all-start.1) | async-done | bytes 196640 | tf_op jit(solution)/shard_map/all_to_all | solution.py:130
  100.5 2.1 fusion.3
  102.6 0.0 all-gather.3.cloned.1.call-update
  102.7 0.2 reduce-scatter.2.cloned.1.call-start
  102.9 106.5 %all-gather.3.cloned.1.call-done = bf16[8,2192,192]{1,2,0:T(8,128)(2,1)} async-done(((bf16[1,2192,192]{1,2,0:T(8,128)(2,1)}), bf16[8,2192,192]{1,2,0:T(8,128)(2,1)}) %all-gather.3.cloned.1.call-update) | async-done | bytes 6733840 | tf_op jit(solution)/shard_map/all_gather | solution.py:142
  209.4 9.8 %copy.26 = bf16[8,2192,192]{1,0,2:T(8,128)(2,1)} copy(bf16[8,2192,192]{1,2,0:T(8,128)(2,1)} %all-gather.3.cloned.1.call-done) | data formatting | bytes 13467648 | tf_op jit(solution)/shard_map/all_gather | solution.py:142
  219.3 12.5 %reshape.97 = bf16[17536,192]{0,1:T(8,128)(2,1)} reshape(bf16[8,2192,192]{1,0,2:T(8,128)(2,1)} %copy.26) | data formatting | bytes 13467648
  231.8 31.1 %convolution_bitcast_fusion = f32[2000,192]{0,1:T(8,128)} fusion(bf16[17536,192]{0,1:T(8,128)(2,1)} %reshape.97, bf16[2000,17536]{1,0:T(8,128)(2,1)} %param.27), kind=kOutput, calls=%fused_computation.10 | convolution fusion | flops 13467648000 | bytes 78413824 | tf_op jit(solution)/shard_map/dot_general | solution.py:140
  262.9 0.0 reduce-scatter.2.cloned.1.call-update
  262.9 26.5 %reduce-scatter.2.cloned.1.call-done = f32[2000,48]{0,1:T(8,128)} async-done(((f32[2000,192]{0,1:T(8,128)}), f32[2000,48]{0,1:T(8,128)}) %reduce-scatter.2.cloned.1.call-update) | async-done | bytes 384016 | tf_op jit(solution)/shard_map/reduce_scatter | solution.py:145
  (11 shorter events, 0.1 us)
Async XLA Ops:
  6.5 35.2 %copy-start.4 = (s32[256]{0:T(256)S(1)}, s32[256]{0:T(256)}, u32[]{:S(2)}) copy-start(s32[256]{0:T(256)} %param.22) | copy-start | bytes 3076
  6.5 42.7 %copy-start.5 = (f32[256]{0:T(256)S(1)}, f32[256]{0:T(256)}, u32[]{:S(2)}) copy-start(f32[256]{0:T(256)} %param.25) | copy-start | bytes 3076
  6.5 42.7 %copy-start.1 = (s32[192,256]{1,0:T(8,128)S(1)}, s32[192,256]{1,0:T(8,128)}, u32[]{:S(2)}) copy-start(s32[192,256]{1,0:T(8,128)} %param.18) | copy-start | bytes 589828
  6.5 42.7 %copy-start.3 = (f32[192,256]{1,0:T(8,128)S(1)}, f32[192,256]{1,0:T(8,128)}, u32[]{:S(2)}) copy-start(f32[192,256]{1,0:T(8,128)} %param.16) | copy-start | bytes 589828
  6.5 42.7 %copy-start = (f32[192,256]{1,0:T(8,128)S(1)}, f32[192,256]{1,0:T(8,128)}, u32[]{:S(2)}) copy-start(f32[192,256]{1,0:T(8,128)} %param.15) | copy-start | bytes 589828
  6.5 42.7 %copy-start.2 = (f32[192,256]{1,0:T(8,128)S(1)}, f32[192,256]{1,0:T(8,128)}, u32[]{:S(2)}) copy-start(f32[192,256]{1,0:T(8,128)} %param.14) | copy-start | bytes 589828
  10.4 73.7 %all-to-all-start = ((s32[1,32,16]{2,0,1:T(1,128)}), s32[1,32,16]{2,0,1:T(1,128)S(1)}, u32[]{:S(2)}, u32[]{:S(2)}) async-start(s32[1,32,16]{2,0,1:T(1,128)} %bitcast.2), calls=%async_computation | async-start | bytes 32768 | tf_op jit(solution)/shard_map/all_to_all | solution.py:131
  84.1 16.4 %all-to-all-start.1 = ((bf16[192,32,16]{0,2,1:T(8,128)(2,1)}), bf16[192,32,16]{0,2,1:T(8,128)(2,1)S(1)}, u32[]{:S(2)}, u32[]{:S(2)}) async-start(bf16[192,32,16]{0,2,1:T(8,128)(2,1)} %bitcast.72), calls=%async_computation.1 | async-start | bytes 524288 | tf_op jit(solution)/shard_map/all_to_all | solution.py:130
  89.9 119.5 %all-gather.3.cloned.1.call-start = ((), (), s32[]{:S(2)}) async-start(), calls=%async_computation.4 | async-start | bytes 7962624 | tf_op jit(solution)/shard_map/all_gather | solution.py:142
  102.7 186.8 %reduce-scatter.2.cloned.1.call-start = ((), (), s32[]{:S(2)}) async-start(), calls=%async_computation.3 | async-start | bytes 1966080 | tf_op jit(solution)/shard_map/reduce_scatter | solution.py:145
Sparse Core Ops, SparseCore 0:
  102.8 106.5 all-gather.2
  263.0 26.3 reduce-scatter.1
where the time goes:
time: 298 us; the launch traced here: 296 us
  waiting for transfers between devices  142 us (48%)
  other arithmetic  50.1 us (17%)
  matrix products  38.8 us (13%)
  local copies, waits for them, and re-layouts  38 us (13%)
  between operations  13.6 us (5%)
  starting transfers between devices  13.4 us (4%)
    all_gather x1, waiting for transfers between devices, per_device(): lax.all_gather(injection, 'line', axis=0, tiled=True)  107 us
    convert_element_type x1, other arithmetic, site_power(): return (site_capacity * plane / 1000.0).astype(jnp.bfloat16)  32.6 us
    dot_general x1, matrix products, per_device(): jnp.dot(transfer_factors, lax.all_gather(injection, 'line', axis=0, tiled...  31.1 us
    reduce_scatter x1, waiting for transfers between devices, per_device(): lax.psum_scatter(partial_flows, 'bus', scatter_dimension=1, tiled=True)  26.5 us
    unnamed x15, local copies, waits for them, and re-layouts  12.8 us
    all_gather x1, local copies, waits for them, and re-layouts, per_device(): lax.all_gather(injection, 'line', axis=0, tiled=True)  9.83 us
    all_to_all x1, waiting for transfers between devices, per_device(): lax.all_to_all(outgoing, ('line', 'bus'), split_axis=1, concat_axis=1, ti...  9.25 us
    add x1, other arithmetic, site_power(): 1.0 + cos_tilt  7.51 us
  transfers between devices with their start and end apart: 4, of which 3 were waited for; matrix products, arithmetic and copies ran while one was open for 23% of the time, Pallas kernels for 0%

commit v1 on v0

--- a/solution.py
+++ b/solution.py
@@ -11,6 +11,27 @@
 albedo = 0.2
 cos_limit = 0.08716
 row_width = 36
+
+
+def collect(value, axis, dim):
+    size, index, rows = (lax.axis_size(axis), lax.axis_index(axis), value.shape[dim])
+    upward = [(i, (i + 1) % size) for i in range(size)]
+    downward = [(i, (i - 1) % size) for i in range(size)]
+    result = jnp.zeros((*value.shape[:dim], size * rows, *value.shape[dim + 1 :]), value.dtype)
+    result = lax.dynamic_update_slice_in_dim(result, value, index * rows, axis=dim)
+    from_left = from_right = value
+    half = size // 2
+    for hop in range(1, half + 1):
+        from_left = lax.ppermute(from_left, axis, upward)
+        result = lax.dynamic_update_slice_in_dim(
+            result, from_left, (index - hop) % size * rows, axis=dim
+        )
+        if hop < size - half:
+            from_right = lax.ppermute(from_right, axis, downward)
+            result = lax.dynamic_update_slice_in_dim(
+                result, from_right, (index + hop) % size * rows, axis=dim
+            )
+    return result
 
 
 def pick_table(classes, table, count):
@@ -138,9 +159,7 @@
         jnp.bfloat16
     )
     partial_flows = jnp.dot(
-        transfer_factors,
-        lax.all_gather(injection, "line", axis=0, tiled=True),
-        preferred_element_type=jnp.float32,
+        transfer_factors, collect(injection, "line", 0), preferred_element_type=jnp.float32
     )
     return lax.psum_scatter(partial_flows, "bus", scatter_dimension=1, tiled=True)
 

time: 298 us -> 362 us (1.21)
  local copies, waits for them, and re-layouts: 38 us -> 88.5 us
  starting transfers between devices: 13.4 us -> 29.9 us
    all_gather x1 -> x0, waiting for transfers between devices: 107 us -> none  [per_device(): lax.all_gather(injection, 'line', axis=0, tiled=True)]
    ppermute x0 -> x7, waiting for transfers between devices: none -> 102 us  [the longest x4 102 us: collect(): from_left = lax.ppermute(from_left, axis, upward)]
    dynamic_update_slice x0 -> x8, local copies, waits for them, and re-layouts: none -> 69.6 us  [the longest x4 34.8 us: collect(): lax.dynamic_update_slice_in_dim(result, from_left, (index - hop) % size *...]
    ppermute x0 -> x7, starting transfers between devices: none -> 16.7 us  [the longest x4 8.38 us: collect(): from_left = lax.ppermute(from_left, axis, upward)]
    unnamed x15 -> x16, local copies, waits for them, and re-layouts: 12.8 us -> 0.23 us
    all_gather x1 -> x0, local copies, waits for them, and re-layouts: 9.83 us -> none  [per_device(): lax.all_gather(injection, 'line', axis=0, tiled=True)]
  transfers between devices with their start and end apart: 4 -> 10, of which waited for: 3 -> 5; matrix products, arithmetic and copies ran while one was open for 23% -> 37% of each run, Pallas kernels for 0% -> 0%
where the time goes in v1:
time: 362 us; the launch traced here: 359 us
  waiting for transfers between devices  139 us (38%)
  local copies, waits for them, and re-layouts  88.5 us (24%)
  other arithmetic  50.1 us (14%)
  matrix products  37.8 us (10%)
  starting transfers between devices  29.9 us (8%)
  between operations  13.6 us (4%)
    ppermute x4, waiting for transfers between devices, collect(): from_left = lax.ppermute(from_left, axis, upward)  102 us
    dynamic_update_slice x4, local copies, waits for them, and re-layouts, collect(): lax.dynamic_update_slice_in_dim(result, from_left, (index - hop) % size *...  34.8 us
    convert_element_type x1, other arithmetic, site_power(): return (site_capacity * plane / 1000.0).astype(jnp.bfloat16)  32.6 us
    dot_general x1, matrix products, per_device(): jnp.dot(transfer_factors, collect(injection, 'line', 0), preferred_elemen...  31.1 us
    reduce_scatter x1, waiting for transfers between devices, per_device(): lax.psum_scatter(partial_flows, 'bus', scatter_dimension=1, tiled=True)  28.3 us
    dynamic_update_slice x3, local copies, waits for them, and re-layouts, collect(): lax.dynamic_update_slice_in_dim(result, from_right, (index + hop) % size...  26.9 us
    all_to_all x1, waiting for transfers between devices, per_device(): lax.all_to_all(outgoing, ('line', 'bus'), split_axis=1, concat_axis=1, ti...  9.14 us
    ppermute x4, starting transfers between devices, collect(): from_left = lax.ppermute(from_left, axis, upward)  8.38 us
  transfers between devices with their start and end apart: 10, of which 5 were waited for; matrix products, arithmetic and copies ran while one was open for 37% of the time, Pallas kernels for 0%

profile of v1, /device:TPU:0, one launch (start us, length us, event | category | flops | bytes accessed | tf_op | source)
XLA Modules:
  0.0 359.1 jit_solution(1913740389737753624)
XLA Ops:
  6.6 0.8 and_select_fusion
  7.3 0.6 reduce-window.6
  7.9 0.2 slice_reduce_fusion
  8.2 0.1 fusion.26
  8.3 1.4 scatter_custom_fusion
  9.7 0.7 all_to_all.14
  10.4 7.3 %all-to-all-start = ((s32[1,32,16]{2,0,1:T(1,128)}), s32[1,32,16]{2,0,1:T(1,128)S(1)}, u32[]{:S(2)}, u32[]{:S(2)}) async-start(s32[1,32,16]{2,0,1:T(1,128)} %bitcast.2), calls=%async_computation | async-start | bytes 32768 | tf_op jit(solution)/shard_map/all_to_all | solution.py:152
  17.7 2.1 fusion.33
  19.8 2.1 fusion.34
  21.9 1.7 fusion.35
  23.6 1.0 remainder_bitcast_fusion
  24.6 1.0 sign_compare_fusion
  25.6 1.6 fusion.37
  27.2 5.7 %fusion.32 = (f32[256]{0:T(256)S(1)}, f32[256]{0:T(256)S(1)}) fusion(f32[]{:T(128)} %bitcast.10, s32[256]{0:T(256)} %param.21, f32[]{:T(128)} %bitcast.9, f32[]{:T(128)} %bitcast.8, f32[]{:T(128)} %bitcast.7, f32[]{:T(128)} %bitcast.6, f32[]{:T(128)} %bitcast.5, f32[]{:T(128)} %bitcast.4, f32[]{:T(128)} %bitcast.3), kind=kLoop, calls=%fused_computation.88 | loop fusion | flops 4096 | bytes 3104 | tf_op jit(solution)/shard_map/sin | solution.py:93
  33.0 1.8 fusion.36
  34.8 0.1 copy.25
  34.9 0.1 copy.26
  35.0 0.8 reshape.70
  35.9 5.6 %fusion.4 = f32[49152]{0:T(1024)S(1)} fusion(f32[35,36]{1,0:T(8,128)S(1)} %reshape.70, s32[49152]{0:T(1024)S(1)} %get-tuple-element.8, s32[49152]{0:T(1024)S(1)} %get-tuple-element.7), kind=kOutput, calls=%fused_computation.11 | convolution fusion | flops 750157824 | bytes 594864 | tf_op jit(solution)/shard_map/dot_general | solution.py:53
  41.6 7.5 %broadcast_add_fusion = (f32[256]{0:T(256)S(1)}, f32[256]{0:T(256)S(1)}, f32[256]{0:T(256)S(1)}) fusion(f32[256]{0:T(256)S(1)} %cos.6, f32[]{:T(128)} %bitcast.22, s32[256]{0:T(256)S(1)} %copy-done.5, f32[]{:T(128)} %bitcast.21, f32[]{:T(128)} %bitcast.20, f32[]{:T(128)} %bitcast.19, f32[]{:T(128)} %bitcast.18, f32[]{:T(128)} %bitcast.17, f32[]{:T(128)} %bitcast.16, ...), kind=kLoop, calls=%fused_computation.87 | loop fusion | flops 6912 | bytes 5168 | tf_op jit(solution)/shard_map/add | solution.py:98
  49.2 32.6 %fusion.24 = bf16[256,192]{0,1:T(8,128)(2,1)S(1)} fusion(f32[256]{0:T(256)S(1)} %get-tuple-element.62, f32[]{:T(128)} %bitcast.70, f32[]{:T(128)} %bitcast.69, f32[]{:T(128)} %bitcast.68, f32[]{:T(128)} %bitcast.67, f32[]{:T(128)} %bitcast.66, f32[]{:T(128)} %bitcast.65, f32[]{:T(128)} %bitcast.64, f32[]{:T(128)} %bitcast.63, f32[]{:T(128)} %bitcast.62, ...), kind=kLoop, calls=%fused_computation.44 | loop fusion | flops 6733824 | bytes 1087680 | tf_op jit(solution)/shard_map/convert_element_type | solution.py:103
  81.8 2.1 scatter_custom_fusion.1
  84.0 5.8 %all-to-all-start.1 = ((bf16[192,32,16]{0,2,1:T(8,128)(2,1)}), bf16[192,32,16]{0,2,1:T(8,128)(2,1)S(1)}, u32[]{:S(2)}, u32[]{:S(2)}) async-start(bf16[192,32,16]{0,2,1:T(8,128)(2,1)} %bitcast.72), calls=%async_computation.1 | async-start | bytes 524288 | tf_op jit(solution)/shard_map/all_to_all | solution.py:151
  89.9 0.6 broadcast.205
  90.5 0.7 reduce.5
  91.3 9.1 %all-to-all-done.1 = bf16[192,32,16]{0,2,1:T(8,128)(2,1)S(1)} async-done(((bf16[192,32,16]{0,2,1:T(8,128)(2,1)}), bf16[192,32,16]{0,2,1:T(8,128)(2,1)S(1)}, u32[]{:S(2)}, u32[]{:S(2)}) %all-to-all-start.1) | async-done | bytes 196640 | tf_op jit(solution)/shard_map/all_to_all | solution.py:151
  100.4 1.2 fusion.2
  101.6 0.9 collective-permute-start
  102.6 3.8 %collective-permute-start.1 = (bf16[2192,192]{0,1:T(8,128)(2,1)S(1)}, bf16[2192,192]{0,1:T(8,128)(2,1)S(1)}, u32[]{:S(2)}, u32[]{:S(2)}) collective-permute-start(bf16[2192,192]{0,1:T(8,128)(2,1)S(1)} %fusion.2), channel_id=1, source_target_pairs={{0,28},{4,0},{8,4},{12,8},{16,12},{20,16},{24,20},{28,24},{1,29},{... | collective-permute-start | bytes 2525192 | tf_op jit(solution)/shard_map/ppermute | solution.py:30
  106.4 33.5 %collective-permute-done = bf16[2192,192]{0,1:T(8,128)(2,1)S(1)} collective-permute-done((bf16[2192,192]{0,1:T(8,128)(2,1)S(1)}, bf16[2192,192]{0,1:T(8,128)(2,1)S(1)}, u32[]{:S(2)}, u32[]{:S(2)}) %collective-permute-start) | collective-permute-done | bytes 841760 | tf_op jit(solution)/shard_map/ppermute | solution.py:25
  139.9 2.5 collective-permute-start.2
  142.4 2.2 collective-permute-start.3
  144.7 34.2 %collective-permute-done.2 = bf16[2192,192]{0,1:T(8,128)(2,1)S(1)} collective-permute-done((bf16[2192,192]{0,1:T(8,128)(2,1)S(1)}, bf16[2192,192]{0,1:T(8,128)(2,1)S(1)}, u32[]{:S(2)}, u32[]{:S(2)}) %collective-permute-start.2) | collective-permute-done | bytes 841760 | tf_op jit(solution)/shard_map/ppermute | solution.py:25
  178.8 2.5 collective-permute-start.4
  181.3 2.2 collective-permute-start.5
  183.6 34.0 %collective-permute-done.4 = bf16[2192,192]{0,1:T(8,128)(2,1)S(1)} collective-permute-done((bf16[2192,192]{0,1:T(8,128)(2,1)S(1)}, bf16[2192,192]{0,1:T(8,128)(2,1)S(1)}, u32[]{:S(2)}, u32[]{:S(2)}) %collective-permute-start.4) | collective-permute-done | bytes 841760 | tf_op jit(solution)/shard_map/ppermute | solution.py:25
  217.6 2.5 collective-permute-start.6
  220.1 3.2 broadcast_in_dim.238
  223.3 7.9 %dynamic_update_slice.24 = bf16[17536,192]{0,1:T(8,128)(2,1)} dynamic-update-slice(bf16[17536,192]{0,1:T(8,128)(2,1)} %broadcast_in_dim.238, bf16[2192,192]{0,1:T(8,128)(2,1)S(1)} %fusion.2, s32[]{:T(128)S(6)} %select_n.382, s32[]{:T(128)} %constant.87.clone.1) | dynamic-update-slice | bytes 1683460 | tf_op jit(solution)/shard_map/dynamic_update_slice | solution.py:21
  231.2 8.0 %dynamic_update_slice.25 = bf16[17536,192]{0,1:T(8,128)(2,1)} dynamic-update-slice(bf16[17536,192]{0,1:T(8,128)(2,1)} %dynamic_update_slice.24, bf16[2192,192]{0,1:T(8,128)(2,1)S(1)} %collective-permute-done, s32[]{:T(128)S(6)} %select_n.384, s32[]{:T(128)} %constant.87.clone.1) | dynamic-update-slice | bytes 1683460 | tf_op jit(solution)/shard_map/dynamic_update_slice | solution.py:26
  239.2 8.7 %dynamic_update_slice.26 = bf16[17536,192]{0,1:T(8,128)(2,1)} dynamic-update-slice(bf16[17536,192]{0,1:T(8,128)(2,1)} %dynamic_update_slice.25, bf16[2192,192]{0,1:T(8,128)(2,1)S(1)} %collective-permute-done.1, s32[]{:T(128)S(6)} %select_n.386, s32[]{:T(128)} %constant.87.clone.1) | dynamic-update-slice | bytes 1683460 | tf_op jit(solution)/shard_map/dynamic_update_slice | solution.py:31
  247.9 9.0 %dynamic_update_slice.27 = bf16[17536,192]{0,1:T(8,128)(2,1)} dynamic-update-slice(bf16[17536,192]{0,1:T(8,128)(2,1)} %dynamic_update_slice.26, bf16[2192,192]{0,1:T(8,128)(2,1)} %copy-done, s32[]{:T(128)S(6)} %select_n.388, s32[]{:T(128)} %constant.87.clone.1) | dynamic-update-slice | bytes 1683460 | tf_op jit(solution)/shard_map/dynamic_update_slice | solution.py:26
  256.9 9.1 %dynamic_update_slice.28 = bf16[17536,192]{0,1:T(8,128)(2,1)} dynamic-update-slice(bf16[17536,192]{0,1:T(8,128)(2,1)} %dynamic_update_slice.27, bf16[2192,192]{0,1:T(8,128)(2,1)} %collective-permute-done.3, s32[]{:T(128)S(6)} %select_n.390, s32[]{:T(128)} %constant.87.clone.1) | dynamic-update-slice | bytes 1683460 | tf_op jit(solution)/shard_map/dynamic_update_slice | solution.py:31
  266.0 8.7 %dynamic_update_slice.29 = bf16[17536,192]{0,1:T(8,128)(2,1)} dynamic-update-slice(bf16[17536,192]{0,1:T(8,128)(2,1)} %dynamic_update_slice.28, bf16[2192,192]{0,1:T(8,128)(2,1)S(1)} %collective-permute-done.4, s32[]{:T(128)S(6)} %select_n.392, s32[]{:T(128)} %constant.87.clone.1) | dynamic-update-slice | bytes 1683460 | tf_op jit(solution)/shard_map/dynamic_update_slice | solution.py:26
  274.7 9.1 %dynamic_update_slice.30 = bf16[17536,192]{0,1:T(8,128)(2,1)} dynamic-update-slice(bf16[17536,192]{0,1:T(8,128)(2,1)} %dynamic_update_slice.29, bf16[2192,192]{0,1:T(8,128)(2,1)} %collective-permute-done.5, s32[]{:T(128)S(6)} %select_n.394, s32[]{:T(128)} %constant.87.clone.1) | dynamic-update-slice | bytes 1683460 | tf_op jit(solution)/shard_map/dynamic_update_slice | solution.py:31
  283.8 9.1 %dynamic_update_slice.31 = bf16[17536,192]{0,1:T(8,128)(2,1)} dynamic-update-slice(bf16[17536,192]{0,1:T(8,128)(2,1)} %dynamic_update_slice.30, bf16[2192,192]{0,1:T(8,128)(2,1)} %collective-permute-done.6, s32[]{:T(128)S(6)} %select_n.396, s32[]{:T(128)} %constant.87.clone.1) | dynamic-update-slice | bytes 1683460 | tf_op jit(solution)/shard_map/dynamic_update_slice | solution.py:26
  292.9 31.1 %convolution_bitcast_fusion = f32[2000,192]{0,1:T(8,128)} fusion(bf16[17536,192]{0,1:T(8,128)(2,1)} %dynamic_update_slice.31, bf16[2000,17536]{1,0:T(8,128)(2,1)} %param.27), kind=kOutput, calls=%fused_computation.9 | convolution fusion | flops 13467648000 | bytes 78413824 | tf_op jit(solution)/shard_map/dot_general | solution.py:161
  324.0 28.3 %reduce-scatter.2.cloned.1.call-done = f32[2000,48]{0,1:T(8,128)} async-done(((f32[2000,192]{0,1:T(8,128)}), f32[2000,48]{0,1:T(8,128)}) %reduce-scatter.2.cloned.1.call-update) | async-done | bytes 384016 | tf_op jit(solution)/shard_map/reduce_scatter | solution.py:164
  (31 shorter events, 0.6 us)
Async XLA Ops:
  6.5 35.0 %copy-start.5 = (s32[256]{0:T(256)S(1)}, s32[256]{0:T(256)}, u32[]{:S(2)}) copy-start(s32[256]{0:T(256)} %param.22) | copy-start | bytes 3076
  6.5 42.6 %copy-start.3 = (f32[192,256]{1,0:T(8,128)S(1)}, f32[192,256]{1,0:T(8,128)}, u32[]{:S(2)}) copy-start(f32[192,256]{1,0:T(8,128)} %param.14) | copy-start | bytes 589828
  6.5 42.6 %copy-start.1 = (f32[192,256]{1,0:T(8,128)S(1)}, f32[192,256]{1,0:T(8,128)}, u32[]{:S(2)}) copy-start(f32[192,256]{1,0:T(8,128)} %param.15) | copy-start | bytes 589828
  6.5 42.6 %copy-start.4 = (f32[192,256]{1,0:T(8,128)S(1)}, f32[192,256]{1,0:T(8,128)}, u32[]{:S(2)}) copy-start(f32[192,256]{1,0:T(8,128)} %param.16) | copy-start | bytes 589828
  6.5 42.6 %copy-start.2 = (s32[192,256]{1,0:T(8,128)S(1)}, s32[192,256]{1,0:T(8,128)}, u32[]{:S(2)}) copy-start(s32[192,256]{1,0:T(8,128)} %param.18) | copy-start | bytes 589828
  6.5 42.6 %copy-start.6 = (f32[256]{0:T(256)S(1)}, f32[256]{0:T(256)}, u32[]{:S(2)}) copy-start(f32[256]{0:T(256)} %param.25) | copy-start | bytes 3076
  10.4 73.6 %all-to-all-start = ((s32[1,32,16]{2,0,1:T(1,128)}), s32[1,32,16]{2,0,1:T(1,128)S(1)}, u32[]{:S(2)}, u32[]{:S(2)}) async-start(s32[1,32,16]{2,0,1:T(1,128)} %bitcast.2), calls=%async_computation | async-start | bytes 32768 | tf_op jit(solution)/shard_map/all_to_all | solution.py:152
  84.0 16.4 %all-to-all-start.1 = ((bf16[192,32,16]{0,2,1:T(8,128)(2,1)}), bf16[192,32,16]{0,2,1:T(8,128)(2,1)S(1)}, u32[]{:S(2)}, u32[]{:S(2)}) async-start(bf16[192,32,16]{0,2,1:T(8,128)(2,1)} %bitcast.72), calls=%async_computation.1 | async-start | bytes 524288 | tf_op jit(solution)/shard_map/all_to_all | solution.py:151
  89.8 262.5 %reduce-scatter.2.cloned.1.call-start = ((), (), s32[]{:S(2)}) async-start(), calls=%async_computation.3 | async-start | bytes 1966080 | tf_op jit(solution)/shard_map/reduce_scatter | solution.py:164
  101.6 38.3 %collective-permute-start = (bf16[2192,192]{0,1:T(8,128)(2,1)S(1)}, bf16[2192,192]{0,1:T(8,128)(2,1)S(1)}, u32[]{:S(2)}, u32[]{:S(2)}) collective-permute-start(bf16[2192,192]{0,1:T(8,128)(2,1)S(1)} %fusion.2), channel_id=1, source_target_pairs={{0,4},{4,8},{8,12},{12,16},{16,20},{20,24},{24,28},{28,0},{1,5},{5... | collective-permute-start | bytes 2525192 | tf_op jit(solution)/shard_map/ppermute | solution.py:25
  102.6 39.8 %collective-permute-start.1 = (bf16[2192,192]{0,1:T(8,128)(2,1)S(1)}, bf16[2192,192]{0,1:T(8,128)(2,1)S(1)}, u32[]{:S(2)}, u32[]{:S(2)}) collective-permute-start(bf16[2192,192]{0,1:T(8,128)(2,1)S(1)} %fusion.2), channel_id=1, source_target_pairs={{0,28},{4,0},{8,4},{12,8},{16,12},{20,16},{24,20},{28,24},{1,29},{... | collective-permute-start | bytes 2525192 | tf_op jit(solution)/shard_map/ppermute | solution.py:30
  139.9 38.9 %collective-permute-start.2 = (bf16[2192,192]{0,1:T(8,128)(2,1)S(1)}, bf16[2192,192]{0,1:T(8,128)(2,1)S(1)}, u32[]{:S(2)}, u32[]{:S(2)}) collective-permute-start(bf16[2192,192]{0,1:T(8,128)(2,1)S(1)} %collective-permute-done), channel_id=1, source_target_pairs={{0,4},{4,8},{8,12},{12,16},{16,20},{20,24},{24,28},{28,0},{1,5},{5... | collective-permute-start | bytes 2525192 | tf_op jit(solution)/shard_map/ppermute | solution.py:25
  142.4 38.9 %collective-permute-start.3 = (bf16[2192,192]{0,1:T(8,128)(2,1)S(1)}, bf16[2192,192]{0,1:T(8,128)(2,1)}, u32[]{:S(2)}, u32[]{:S(2)}) collective-permute-start(bf16[2192,192]{0,1:T(8,128)(2,1)S(1)} %collective-permute-done.1), channel_id=1, source_target_pairs={{0,28},{4,0},{8,4},{12,8},{16,12},{20,16},{24,20},{28,24},{1,29},{... | collective-permute-start | bytes 2525192 | tf_op jit(solution)/shard_map/ppermute | solution.py:30
  178.8 38.8 %copy-start = (bf16[2192,192]{0,1:T(8,128)(2,1)}, bf16[2192,192]{0,1:T(8,128)(2,1)S(1)}, u32[]{:S(2)}) copy-start(bf16[2192,192]{0,1:T(8,128)(2,1)S(1)} %collective-permute-done.2) | copy-start | bytes 2525188
  178.8 38.8 %collective-permute-start.4 = (bf16[2192,192]{0,1:T(8,128)(2,1)S(1)}, bf16[2192,192]{0,1:T(8,128)(2,1)S(1)}, u32[]{:S(2)}, u32[]{:S(2)}) collective-permute-start(bf16[2192,192]{0,1:T(8,128)(2,1)S(1)} %collective-permute-done.2), channel_id=1, source_target_pairs={{0,4},{4,8},{8,12},{12,16},{16,20},{20,24},{24,28},{28,0},{1,5},{5... | collective-permute-start | bytes 2525192 | tf_op jit(solution)/shard_map/ppermute | solution.py:25
  181.3 93.4 %collective-permute-start.5 = (bf16[2192,192]{0,1:T(8,128)(2,1)}, bf16[2192,192]{0,1:T(8,128)(2,1)}, u32[]{:S(2)}, u32[]{:S(2)}) collective-permute-start(bf16[2192,192]{0,1:T(8,128)(2,1)} %collective-permute-done.3), channel_id=1, source_target_pairs={{0,28},{4,0},{8,4},{12,8},{16,12},{20,16},{24,20},{28,24},{1,29},{... | collective-permute-start | bytes 2525192 | tf_op jit(solution)/shard_map/ppermute | solution.py:30
  217.6 66.2 %collective-permute-start.6 = (bf16[2192,192]{0,1:T(8,128)(2,1)S(1)}, bf16[2192,192]{0,1:T(8,128)(2,1)}, u32[]{:S(2)}, u32[]{:S(2)}) collective-permute-start(bf16[2192,192]{0,1:T(8,128)(2,1)S(1)} %collective-permute-done.4), channel_id=1, source_target_pairs={{0,4},{4,8},{8,12},{12,16},{16,20},{20,24},{24,28},{28,0},{1,5},{5... | collective-permute-start | bytes 2525192 | tf_op jit(solution)/shard_map/ppermute | solution.py:25
Sparse Core Ops, SparseCore 0:
  324.1 28.1 reduce-scatter.1
